TPU v7x, 32 devices: a whole 2x2x4 slice. The times are simulated.
32 devices in a mesh: tile: 8 (over z, y), band: 4 (over x, core).
Axes of the slice: x: 2, y: 2, z: 4, core: 2. Of those that a mesh axis runs over, the one named last changes fastest.
Arguments:
- calib: bfloat16 [16, 8, 64, 8192], P('tile', None, None, 'band'), may hold values from -0.09375 to 0.09375
- support: int32 [16, 8], P('tile'), may hold values from 0 to 15, as said below
- band_window: int32 [16, 8, 2], P('tile'), may hold values from 0 to 128, as said below
- measured: float32 [1024], P('tile'), may hold values from -60 to 60
Outputs:
- solution: float32 [16, 8192], P('tile', 'band')
- residual: float32 [1024], P('tile')
Inputs may be any that keep to these rules, and one draw needn't show every extreme that they name: `support`: entries 0 to 3 of each tile name blocks within 4 of the tile's own number along the cyclic order; the other entries name blocks whose index of tile (block // 2) lies 3 to 8 - 3 steps ahead of the tile's own, cyclically, and the tiles of one index of tile name at most 3 such blocks of any one other index. `band_window`: each window holds at least a quarter of the 128 bands; the first band is at most half of 128.
All inputs are finite; a program needn't handle non-finite values.
Results may differ from a plain program's by a relative error of at most 0.012.
The roundings to bfloat16 on the way count: a program that leaves them out, or rounds other values in their place, can miss the bound.
Values may be sent and summed in bfloat16 or wider, within the bound.
A program may use at most 64 MiB of HBM per device.

v0:
```python
import jax
import jax.numpy as jnp
from jax import lax
from jax.sharding import PartitionSpec as P

PIX = 64
ITERS = 2


ridge_weight = 0.25


def band_mask(band_window, width):
    slab = width // PIX
    bands = lax.axis_index("band") * slab + jnp.arange(width, dtype=jnp.int32) // PIX
    lower = band_window[:, :, 0][:, :, None]
    upper = band_window[:, :, 1][:, :, None]
    return (bands[None, None, :] >= lower) & (bands[None, None, :] < upper)


def grad_square(local_part):
    return lax.psum(jnp.sum(local_part * local_part), ("tile", "band"))


def body(calib, support, band_window, measured):
    tile_rows = calib.shape[0]
    width = calib.shape[3]
    entries = support.reshape(-1)
    inside = band_mask(band_window, width)

    def adjoint(sensor_b):
        terms = jnp.einsum(
            "tkij,ti->tkj",
            calib,
            sensor_b.reshape(tile_rows, calib.shape[2]),
            preferred_element_type=jnp.float32,
        )
        terms = jnp.where(inside, terms, jnp.zeros((), jnp.float32))
        terms = terms.reshape(-1, width)
        rows = jnp.arange(tile_rows * lax.axis_size("tile"), dtype=jnp.int32)
        place = (rows[:, None] == entries[None, :]).astype(jnp.float32)
        return lax.psum_scatter(
            jnp.dot(
                place, terms, precision=lax.Precision.HIGHEST, preferred_element_type=jnp.float32
            ),
            "tile",
            scatter_dimension=0,
            tiled=True,
        )

    residual = measured
    gradient = adjoint(measured.astype(jnp.bfloat16))
    direction = gradient
    solution = jnp.zeros_like(gradient)
    gamma = grad_square(gradient)
    for step in range(ITERS):
        packed = direction.astype(jnp.bfloat16)
        piece = lax.all_gather(packed, "tile", axis=0, tiled=True)
        select = (entries[:, None] == jnp.arange(piece.shape[0], dtype=jnp.int32)[None, :]).astype(
            jnp.bfloat16
        )
        picked = jnp.dot(select, piece, preferred_element_type=jnp.float32).astype(jnp.bfloat16)
        chosen = jnp.where(inside, picked.reshape(inside.shape), jnp.zeros((), jnp.bfloat16))
        values = jnp.einsum("tkij,tkj->ti", calib, chosen, preferred_element_type=jnp.float32)
        partial_image = values.reshape(-1)
        mine = direction
        image = lax.psum(partial_image, "band")
        image_sq = lax.psum(jnp.sum(image * image), "tile")
        direction_sq = lax.psum(jnp.sum(mine * mine), ("tile", "band"))
        delta = image_sq + ridge_weight * direction_sq
        alpha = gamma / delta
        solution = solution + alpha * direction
        residual = residual - alpha * image
        if step + 1 < ITERS:
            sensor_b = residual.astype(jnp.bfloat16)
            gradient = adjoint(sensor_b) - ridge_weight * solution
            gamma_next = grad_square(gradient)
            direction = gradient + gamma_next / gamma * direction
            gamma = gamma_next
    return (solution, residual)


def solution(mesh):
    placed = (P("tile", None, None, "band"), P("tile", None), P("tile", None, None), P("tile"))
    return jax.shard_map(
        body, mesh=mesh, in_specs=placed, out_specs=(P("tile", "band"), P("tile")), check_vma=False
    )
```

profile of v0, /device:TPU:0, one launch (start us, length us, event | category | flops | bytes accessed | tf_op | source)
XLA Modules:
  0.0 418.5 jit_solution(17100222713692962372)
XLA Ops:
  7.2 0.0 copy-start.2
  7.2 0.0 all-reduce.5.cloned.1.call-start
  7.2 0.8 eq.15
  8.0 0.7 convert_element_type.22
  8.6 0.1 reshape.65
  8.7 0.8 fusion.29
  9.5 0.0 copy-start.1
  9.5 2.9 fusion.30
  12.4 0.9 fusion.8
  13.3 0.0 all-reduce.5.cloned.1.call-update
  13.4 0.0 all-reduce.7.cloned.1.call-start
  13.4 0.0 copy-done.2
  13.4 0.6 dynamic-slice
  14.7 71.9 %all-reduce.5.cloned.1.call-done = f32[16,2048]{1,0:T(8,128)} async-done(((f32[16,2048]{1,0:T(8,128)}), f32[16,2048]{1,0:T(8,128)}) %all-reduce.5.cloned.1.call-update) | async-done | bytes 131088
  86.6 0.0 copy-start
  86.6 0.9 convert_bitcast_fusion.1
  87.5 30.5 %all-gather = bf16[8,2,2048]{2,1,0:T(2,128)(2,1)S(1)} all-gather(bf16[1,2,2048]{2,1,0:T(2,128)(2,1)S(1)} %convert_bitcast_fusion.1), channel_id=1, replica_groups=mesh['tile'=8,'band'=4] {'tile'}, dimensions={0}, use_global_device_ids=true | all-gather | bytes 73728 | tf_op jit(solution)/shard_map/all_gather | solution.py:58
  118.1 0.2 fusion.5
  118.3 3.4 fusion.13
  121.7 0.1 reshape.47
  121.8 5.6 %psum.53 = f32[128]{0:T(128)S(1)} all-reduce(f32[128]{0:T(128)S(1)} %reshape.47), channel_id=1, replica_groups=mesh['tile'=8,'band'=4] {'band'}, use_global_device_ids=true, to_apply=%region_3.4 | all-reduce | flops 128 | bytes 1024 | tf_op jit(solution)/shard_map/psum | solution.py:67
  127.5 0.0 copy-done
  127.5 0.6 multiply_reduce_fusion.2
  128.1 0.6 multiply_reduce_fusion.4
  128.7 38.2 %psum.52 = f32[]{:T(128)} all-reduce(f32[]{:T(128)} %multiply_reduce_fusion.2), channel_id=1, replica_groups=mesh['tile'=8,'band'=4] {'tile','band'}, use_global_device_ids=true, to_apply=%region_2.3 | all-reduce | flops 1 | bytes 8 | tf_op jit(solution)/shard_map/psum | solution.py:22
  166.9 21.2 %psum.54 = f32[]{:T(128)} all-reduce(f32[]{:T(128)} %multiply_reduce_fusion.4), channel_id=1, replica_groups=mesh['tile'=8,'band'=4] {'tile'}, use_global_device_ids=true, to_apply=%region_5.6 | all-reduce | flops 1 | bytes 8 | tf_op jit(solution)/shard_map/psum | solution.py:68
  190.0 0.0 copy-done.1
  190.0 0.1 reshape.67
  190.1 2.8 fusion.31
  192.9 0.9 fusion.6
  193.9 0.0 all-reduce.7.cloned.1.call-update
  193.9 67.7 %all-reduce.7.cloned.1.call-done = f32[16,2048]{1,0:T(8,128)} async-done(((f32[16,2048]{1,0:T(8,128)}), f32[16,2048]{1,0:T(8,128)}) %all-reduce.7.cloned.1.call-update) | async-done | bytes 131088
  261.6 1.5 multiply_reduce_fusion.1
  263.0 39.6 %psum.55 = f32[]{:T(128)} all-reduce(f32[]{:T(128)} %multiply_reduce_fusion.1), channel_id=1, replica_groups=mesh['tile'=8,'band'=4] {'tile','band'}, use_global_device_ids=true, to_apply=%region_8.9 | all-reduce | flops 1 | bytes 8 | tf_op jit(solution)/shard_map/psum | solution.py:22
  304.0 1.5 multiply_reduce_fusion
  305.5 40.1 %psum.58 = f32[]{:T(128)} all-reduce(f32[]{:T(128)} %get-tuple-element.2), channel_id=1, replica_groups=mesh['tile'=8,'band'=4] {'tile','band'}, use_global_device_ids=true, to_apply=%region_13.14 | all-reduce | flops 1 | bytes 8 | tf_op jit(solution)/shard_map/psum | solution.py:69
  345.6 30.5 %all-gather.1 = bf16[8,2,2048]{2,1,0:T(2,128)(2,1)S(1)} all-gather(bf16[1,2,2048]{2,1,0:T(2,128)(2,1)S(1)} %convert_bitcast_fusion), channel_id=1, replica_groups=mesh['tile'=8,'band'=4] {'tile'}, dimensions={0}, use_global_device_ids=true | all-gather | bytes 73728 | tf_op jit(solution)/shard_map/all_gather | solution.py:58
  376.2 0.2 fusion.3
  376.4 3.4 fusion.10
  379.8 0.1 reshape.51
  379.9 5.8 %psum.56 = f32[128]{0:T(128)S(1)} all-reduce(f32[128]{0:T(128)S(1)} %reshape.51), channel_id=1, replica_groups=mesh['tile'=8,'band'=4] {'band'}, use_global_device_ids=true, to_apply=%region_9.10 | all-reduce | flops 128 | bytes 1024 | tf_op jit(solution)/shard_map/psum | solution.py:67
  385.7 0.6 multiply_reduce_fusion.3
  387.0 22.1 %psum.57 = f32[]{:T(128)} all-reduce(f32[]{:T(128)} %multiply_reduce_fusion.3), channel_id=1, replica_groups=mesh['tile'=8,'band'=4] {'tile'}, use_global_device_ids=true, to_apply=%region_11.12 | all-reduce | flops 1 | bytes 8 | tf_op jit(solution)/shard_map/psum | solution.py:68
  410.5 0.5 multiply_subtract_fusion
  411.0 0.6 multiply_add_fusion
  (5 shorter events, 0.1 us)
Async XLA Ops:
  7.2 6.3 %copy-start.2 = (u32[32]{0:T(128)S(1)}, u32[32]{0:T(128)}, u32[]{:S(2)}) copy-start(u32[32]{0:T(128)} %constant.36) | copy-start | bytes 388
  7.2 79.4 %all-reduce.5.cloned.1.call-start = ((), (), s32[]{:S(2)}) async-start(), calls=%async_computation | async-start | bytes 262144
  9.5 180.5 %copy-start.1 = (f32[128]{0:T(128)S(1)}, f32[128]{0:T(128)}, u32[]{:S(2)}) copy-start(f32[128]{0:T(128)} %param.7) | copy-start | bytes 1540
  13.4 248.2 %all-reduce.7.cloned.1.call-start = ((), (), s32[]{:S(2)}) async-start(), calls=%async_computation.1 | async-start | bytes 262144
  86.6 40.9 %copy-start = (f32[16,2048]{1,0:T(8,128)S(1)}, f32[16,2048]{1,0:T(8,128)}, u32[]{:S(2)}) copy-start(f32[16,2048]{1,0:T(8,128)} %all-reduce.5.cloned.1.call-done) | copy-start | bytes 393220
Sparse Core Ops, SparseCore 0:
  13.5 73.0 all-reduce.4
  194.0 67.5 all-reduce.6
where the time goes:
time: 419 us; the launch traced here: 418 us
  blocking collectives  234 us (56%)
  waiting for transfers between devices  140 us (33%)
  between operations  20.1 us (5%)
  matrix products  14.9 us (4%)
  other arithmetic  6.58 us (2%)
    unnamed x4, waiting for transfers between devices  140 us
    psum x2, blocking collectives, grad_square(): return lax.psum(jnp.sum(local_part * local_part), ('tile', 'band'))  77.8 us
    all_gather x2, blocking collectives, body(): piece = lax.all_gather(packed, 'tile', axis=0, tiled=True)  61.1 us
    psum x2, blocking collectives, body(): image_sq = lax.psum(jnp.sum(image * image), 'tile')  43.3 us
    psum x1, blocking collectives, body(): direction_sq = lax.psum(jnp.sum(mine * mine), ('tile', 'band'))  40.1 us
    psum x2, blocking collectives, body(): image = lax.psum(partial_image, 'band')  11.5 us
  transfers between devices with their start and end apart: 2, of which 2 were waited for; matrix products, arithmetic and copies ran while one was open for 0% of the time, Pallas kernels for 0%

commit v1 on v0

v1 whole, which is shorter than its diff:
```python
import functools

import jax
import jax.numpy as jnp
from jax import lax
from jax.experimental import pallas as pl
from jax.experimental.pallas import tpu as pltpu
from jax.sharding import PartitionSpec as P

BANDS_PER_GROUP_PIX = 64
RIDGE = 0.25
LANES = 128
RS_TYPE = jnp.float32
MESH = pl.DeviceIdType.MESH


def kernel(
    n_tile,
    n_band,
    group,
    calib,
    support,
    window,
    measured,
    solution_out,
    residual_out,
    held,
    stage,
    rs_buf,
    ag_mine,
    ag_buf,
    sc_mine,
    sc_buf,
    blocks,
    band_buf,
    sq_mine,
    sq_buf,
    load_sem,
    tile_send,
    tile_recv,
    band_send,
    band_recv,
):
    tile_rows, k, pix, width = calib.shape
    entries = tile_rows * k
    rows = entries * pix
    n_block = n_tile * tile_rows
    me = lax.axis_index("tile")
    band = lax.axis_index("band")
    f32 = jnp.float32

    def entry_of(e):
        return e // k, e % k

    loads = []
    for e in range(entries):
        t, j = entry_of(e)
        copy = pltpu.make_async_copy(
            calib.at[t, j], held.at[pl.ds(e * pix, pix), :], load_sem.at[e]
        )
        copy.start()
        loads.append(copy)

    barrier = pltpu.get_barrier_semaphore()
    peers = [lax.rem(me + h, n_tile) for h in range(n_tile)]
    others = [lax.rem(band + h, n_band) for h in range(n_band)]
    for h in range(1, n_tile):
        pl.semaphore_signal(barrier, inc=1, device_id={"tile": peers[h]}, device_id_type=MESH)
    for h in range(1, n_band):
        pl.semaphore_signal(barrier, inc=1, device_id={"band": others[h]}, device_id_type=MESH)

    lane_entry = lax.broadcasted_iota(jnp.int32, (1, rows), 1) // pix
    sup_row = jnp.zeros((1, rows), jnp.int32)
    for e in range(entries):
        t, j = entry_of(e)
        sup_row = jnp.where(lane_entry == e, support[t, j], sup_row)
    slot = lax.broadcasted_iota(jnp.int32, (n_block, 1), 0)
    hop, part = slot // tile_rows, slot % tile_rows
    ahead = me + hop
    ahead = jnp.where(ahead >= n_tile, ahead - n_tile, ahead) * tile_rows + part
    behind = me - hop
    behind = jnp.where(behind < 0, behind + n_tile, behind) * tile_rows + part
    to_adj = jnp.broadcast_to(sup_row, (n_block, rows)) == ahead
    to_fwd = jnp.broadcast_to(sup_row, (n_block, rows)) == behind

    lane = lax.broadcasted_iota(jnp.int32, (1, LANES), 1)
    low = lane < pix

    def spread(w):
        pieces = []
        for t in range(tile_rows):
            col = t * pix // LANES * LANES
            tilev = w[:, col : col + LANES]
            rolled = pltpu.roll(tilev, pix, 1)
            both = jnp.where(low, tilev, rolled) if t * pix % LANES == 0 else jnp.where(low, rolled, tilev)
            pieces += [both] * (k * pix // LANES)
        return jnp.concatenate(pieces, axis=1)

    def left_side(w):
        wide = jnp.broadcast_to(spread(w), (n_block, rows))
        return jnp.where(to_adj, wide, jnp.zeros((), f32)).astype(jnp.bfloat16)

    def exchange_tile(phase, source, target):
        copies = []
        for h in range(1, n_tile):
            copy = pltpu.make_async_remote_copy(
                src_ref=source(h),
                dst_ref=target(h),
                send_sem=tile_send.at[phase, h],
                recv_sem=tile_recv.at[phase, h],
                device_id={"tile": peers[h]},
                device_id_type=MESH,
            )
            copy.start()
            copies.append(copy)
        return copies

    def exchange_band(phase):
        copies = []
        for h in range(1, n_band):
            copy = pltpu.make_async_remote_copy(
                src_ref=band_buf.at[phase, band],
                dst_ref=band_buf.at[phase, band],
                send_sem=band_send.at[phase, h],
                recv_sem=band_recv.at[phase, h],
                device_id={"band": others[h]},
                device_id_type=MESH,
            )
            copy.start()
            copies.append(copy)
        return copies

    def finish(copies):
        for copy in copies:
            copy.wait()

    def scatter_sum(it, phase, product):
        for h in range(n_tile):
            stage[it, h] = product[h * tile_rows : (h + 1) * tile_rows, :].astype(RS_TYPE)
        if it == 0:
            pl.semaphore_wait(barrier, n_tile + n_band - 2)
        copies = exchange_tile(phase, lambda h: stage.at[it, h], lambda h: rs_buf.at[it, h])
        total = product[0:tile_rows, :]
        for h, copy in enumerate(copies, 1):
            copy.wait()
            total = total + rs_buf[it, h].astype(f32)
        return total

    def lanes_sum(x):
        x = jnp.sum(x, axis=0, keepdims=True)
        total = x[:, 0:LANES]
        for c in range(1, width // LANES):
            total = total + x[:, c * LANES : (c + 1) * LANES]
        return total

    def gather_forward(it, phase, vector, scalars):
        packed = vector.astype(jnp.bfloat16)
        ag_mine[it] = packed
        first = exchange_tile(phase, lambda h: ag_mine.at[it], lambda h: ag_buf.at[it, h])
        for i, s in enumerate(scalars):
            sc_mine[it, i : i + 1, :] = s
        second = exchange_tile(phase + 1, lambda h: sc_mine.at[it], lambda h: sc_buf.at[it, h])
        blocks[0:tile_rows, :] = packed.astype(f32)
        for h, copy in enumerate(first, 1):
            copy.wait()
            blocks[h * tile_rows : (h + 1) * tile_rows, :] = ag_buf[it, h].astype(f32)
        out = lax.dot_general(
            blocks[...].astype(jnp.bfloat16),
            held[...],
            (((1,), (1,)), ((), ())),
            preferred_element_type=f32,
        )
        out = jnp.sum(jnp.where(to_fwd, out, jnp.zeros((), f32)), axis=0, keepdims=True)
        cols = []
        per = k * pix // LANES
        for t in range(tile_rows):
            acc = out[:, t * per * LANES : t * per * LANES + LANES]
            for c in range(1, per):
                at = (t * per + c) * LANES
                acc = acc + out[:, at : at + LANES]
            cols.append(acc + pltpu.roll(acc, pix, 1))
        image = jnp.concatenate(
            [jnp.where(low, cols[t], cols[t + 1]) for t in range(0, tile_rows, 2)], axis=1
        )
        finish(second)
        sums = sc_mine[it]
        for h in range(1, n_tile):
            sums = sums + sc_buf[it, h]
        band_buf[it, band, 0:1, :] = image
        band_buf[it, band, 1:3, :] = sums[0:2, :]
        finish(exchange_band(it))
        total = band_buf[it, 0]
        for b in range(1, n_band):
            total = total + band_buf[it, b]
        return total[0:1, :], [jnp.sum(total[i : i + 1, :], axis=1, keepdims=True) for i in (1, 2)]

    def image_square(it, phase, image):
        sq_mine[it, 0:1, :] = image * image
        copies = exchange_tile(phase, lambda h: sq_mine.at[it], lambda h: sq_buf.at[it, h])
        total = image * image
        for h, copy in enumerate(copies, 1):
            copy.wait()
            total = total + sq_buf[it, h, 0:1, :]
        return jnp.sum(total, axis=1, keepdims=True)

    for it in range(2):
        sc_mine[it] = jnp.zeros_like(sc_mine[it])
        sq_mine[it] = jnp.zeros_like(sq_mine[it])
        band_buf[it, band] = jnp.zeros_like(band_buf[it, band])

    start = measured[...]
    left = left_side(start)
    bands = band * (width // BANDS_PER_GROUP_PIX) + (
        lax.broadcasted_iota(jnp.int32, (1, width), 1) // BANDS_PER_GROUP_PIX
    )
    product = jnp.zeros((n_block, width), f32)
    for g in range(entries // group):
        for e in range(g * group, (g + 1) * group):
            t, j = entry_of(e)
            loads[e].wait()
            at = pl.ds(e * pix, pix)
            inside = jnp.where(
                (bands >= window[t, j, 0]) & (bands < window[t, j, 1]), 1.0, 0.0
            ).astype(jnp.bfloat16)
            held[at, :] = held[at, :] * inside
        span = group * pix
        product = product + jnp.dot(
            left[:, g * span : (g + 1) * span],
            held[g * span : (g + 1) * span, :],
            preferred_element_type=f32,
        )
    direction = scatter_sum(0, 0, product)

    norm = lanes_sum(direction * direction)
    image, (gamma, _) = gather_forward(0, 1, direction, [norm])
    alpha = gamma / (image_square(0, 3, image) + RIDGE * gamma)
    solved = alpha * direction
    residual = start - alpha * image

    product = jnp.dot(left_side(residual), held[...], preferred_element_type=f32)
    gradient = scatter_sum(1, 4, product) - RIDGE * solved
    partial, (gamma_next, cross) = gather_forward(
        1, 5, gradient, [lanes_sum(gradient * gradient), lanes_sum(gradient * direction)]
    )
    beta = gamma_next / gamma
    image = partial + beta * image
    square = gamma_next + 2.0 * beta * cross + beta * beta * gamma
    alpha = gamma_next / (image_square(1, 7, image) + RIDGE * square)
    solution_out[...] = solved + alpha * (gradient + beta * direction)
    residual_out[...] = residual - alpha * image


def body(calib, support, band_window, measured):
    n_tile, n_band = lax.axis_size("tile"), lax.axis_size("band")
    tile_rows, k, pix, width = calib.shape
    entries = tile_rows * k
    sensor = tile_rows * pix
    f32, bf16 = jnp.float32, jnp.bfloat16
    vmem, smem = pl.BlockSpec(memory_space=pltpu.VMEM), pl.BlockSpec(memory_space=pltpu.SMEM)
    dma = pltpu.SemaphoreType.DMA
    solved, residual = pl.pallas_call(
        functools.partial(kernel, n_tile, n_band, 4),
        out_shape=(
            jax.ShapeDtypeStruct((tile_rows, width), f32),
            jax.ShapeDtypeStruct((1, sensor), f32),
        ),
        in_specs=[pl.BlockSpec(memory_space=pl.ANY), smem, smem, vmem],
        out_specs=(vmem, vmem),
        scratch_shapes=[
            pltpu.VMEM((entries * pix, width), bf16),
            pltpu.VMEM((2, n_tile, tile_rows, width), RS_TYPE),
            pltpu.VMEM((2, n_tile, tile_rows, width), RS_TYPE),
            pltpu.VMEM((2, tile_rows, width), bf16),
            pltpu.VMEM((2, n_tile, tile_rows, width), bf16),
            pltpu.VMEM((2, 8, LANES), f32),
            pltpu.VMEM((2, n_tile, 8, LANES), f32),
            pltpu.VMEM((n_tile * tile_rows, width), f32),
            pltpu.VMEM((2, n_band, 8, sensor), f32),
            pltpu.VMEM((2, 8, sensor), f32),
            pltpu.VMEM((2, n_tile, 8, sensor), f32),
            dma((entries,)),
            dma((8, n_tile)),
            dma((8, n_tile)),
            dma((2, n_band)),
            dma((2, n_band)),
        ],
        compiler_params=pltpu.CompilerParams(collective_id=0, has_side_effects=True),
    )(calib, support, band_window, measured.reshape(1, sensor))
    return solved, residual.reshape(sensor)


def solution(mesh):
    placed = (P("tile", None, None, "band"), P("tile", None), P("tile", None, None), P("tile"))
    return jax.shard_map(
        body, mesh=mesh, in_specs=placed, out_specs=(P("tile", "band"), P("tile")), check_vma=False
    )
```

time: 419 us -> 48.5 us (0.12)
  blocking collectives: 234 us -> 0 us
  waiting for transfers between devices: 140 us -> 0 us
  Pallas kernels: 0 us -> 43.7 us
  between operations: 20.1 us -> 0.64 us
  matrix products: 14.9 us -> 0 us
  other arithmetic: 6.58 us -> 0 us
    psum x7 -> x0, blocking collectives: 173 us -> none  [the longest x2 77.8 us: grad_square(): return lax.psum(jnp.sum(local_part * local_part), ('tile', 'band'))]
    unnamed x4 -> x0, waiting for transfers between devices: 140 us -> none
    all_gather x2 -> x0, blocking collectives: 61.1 us -> none  [body(): piece = lax.all_gather(packed, 'tile', axis=0, tiled=True)]
    pallas_call x0 -> x1, Pallas kernels: none -> 43.7 us  [body(): pl.pallas_call(functools.partial(kernel, n_tile, n_band, 4), out_shape=(j...]
    dot_general x8 -> x0, matrix products: 14.9 us -> none  [the longest x2 6.81 us: body(): jnp.einsum('tkij,tkj->ti', calib, chosen, preferred_element_type=jnp.floa...]
    reduce_sum x5 -> x0, other arithmetic: 4.77 us -> none  [the longest x2 2.09 us: grad_square(): return lax.psum(jnp.sum(local_part * local_part), ('tile', 'band'))]
  transfers between devices with their start and end apart: 2 -> 0, of which waited for: 2 -> 0; matrix products, arithmetic and copies ran while one was open for 0% -> 0% of each run, Pallas kernels for 0% -> 0%
where the time goes in v1:
time: 48.5 us; the launch traced here: 48.2 us
  Pallas kernels  43.7 us (90%)
  local copies, waits for them, and re-layouts  3.82 us (8%)
  between operations  0.64 us (1%)
    pallas_call x1, Pallas kernels, body(): pl.pallas_call(functools.partial(kernel, n_tile, n_band, 4), out_shape=(j...  43.7 us
    unnamed x3, local copies, waits for them, and re-layouts  3.82 us

profile of v1, /device:TPU:0, one launch (start us, length us, event | category | flops | bytes accessed | tf_op | source)
XLA Modules:
  0.0 48.2 jit_solution(17209787554690913680)
XLA Ops:
  0.6 1.4 %copy.6.window = s32[2,8,2]{2,1,0:T(8,128)} copy(s32[2,8,2]{1,2,0:T(2,128)} %param.6) | data formatting | bytes 256 | tf_op args[2]
  2.0 43.7 %shard_map.59 = (f32[2,2048]{1,0:T(2,128)}, f32[1,128]{1,0:T(1,128)}) custom-call(bf16[2,8,64,2048]{3,2,1,0:T(8,128)(2,1)} %calib.1, s32[2,8]{1,0:T(2,128)} %support.1, s32[2,8,2]{2,1,0:T(8,128)} %copy.6.window, f32[1,128]{1,0:T(1,128)} %bitcast.2), custom_call_target="tpu_custom_call" | custom-call | tf_op jit(solution)/shard_map/pallas_call | solution.py:261
  45.7 1.3 %copy.9 = f32[2,2048]{1,0:T(2,128)} copy(f32[2,2048]{1,0:T(2,128)} %get-tuple-element.8) | data formatting | bytes 32768
  47.1 1.1 %copy.10 = f32[128]{0:T(128)} copy(f32[128]{0:T(128)} %bitcast.3) | data formatting | bytes 1024

commit v2 on v1

--- a/solution.py
+++ b/solution.py
@@ -10,32 +10,39 @@
 BANDS_PER_GROUP_PIX = 64
 RIDGE = 0.25
 LANES = 128
-RS_TYPE = jnp.float32
+RS_TYPES = (jnp.float32, jnp.bfloat16)
+CHUNKS = 4
 MESH = pl.DeviceIdType.MESH
 
 
 def kernel(
     n_tile,
     n_band,
-    group,
     calib,
     support,
     window,
     measured,
-    solution_out,
+    solved_out,
+    step_out,
     residual_out,
+    change_out,
     held,
-    stage,
-    rs_buf,
+    stage_a,
+    stage_b,
+    rs_a,
+    rs_b,
+    product_own,
+    grad_buf,
     ag_mine,
     ag_buf,
     sc_mine,
     sc_buf,
-    blocks,
     band_buf,
     sq_mine,
     sq_buf,
     load_sem,
+    chunk_send,
+    chunk_recv,
     tile_send,
     tile_recv,
     band_send,
@@ -52,14 +59,21 @@
     def entry_of(e):
         return e // k, e % k
 
+    span = width // CHUNKS
+    stage, rs_buf = (stage_a, stage_b), (rs_a, rs_b)
+
     loads = []
-    for e in range(entries):
-        t, j = entry_of(e)
-        copy = pltpu.make_async_copy(
-            calib.at[t, j], held.at[pl.ds(e * pix, pix), :], load_sem.at[e]
-        )
-        copy.start()
-        loads.append(copy)
+    for c in range(CHUNKS):
+        cols = pl.ds(c * span, span)
+        copies = []
+        for e in range(entries):
+            t, j = entry_of(e)
+            copy = pltpu.make_async_copy(
+                calib.at[t, j, :, cols], held.at[c, pl.ds(e * pix, pix), :], load_sem.at[c, e]
+            )
+            copy.start()
+            copies.append(copy)
+        loads.append(copies)
 
     barrier = pltpu.get_barrier_semaphore()
     peers = [lax.rem(me + h, n_tile) for h in range(n_tile)]
@@ -100,14 +114,14 @@
         wide = jnp.broadcast_to(spread(w), (n_block, rows))
         return jnp.where(to_adj, wide, jnp.zeros((), f32)).astype(jnp.bfloat16)
 
-    def exchange_tile(phase, source, target):
+    def exchange_tile(phase, source, target, sends=tile_send, recvs=tile_recv):
         copies = []
         for h in range(1, n_tile):
             copy = pltpu.make_async_remote_copy(
                 src_ref=source(h),
                 dst_ref=target(h),
-                send_sem=tile_send.at[phase, h],
-                recv_sem=tile_recv.at[phase, h],
+                send_sem=sends.at[phase, h],
+                recv_sem=recvs.at[phase, h],
                 device_id={"tile": peers[h]},
                 device_id_type=MESH,
             )
@@ -134,42 +148,58 @@
         for copy in copies:
             copy.wait()
 
-    def scatter_sum(it, phase, product):
+    def scatter_send(it, c, product):
         for h in range(n_tile):
-            stage[it, h] = product[h * tile_rows : (h + 1) * tile_rows, :].astype(RS_TYPE)
-        if it == 0:
-            pl.semaphore_wait(barrier, n_tile + n_band - 2)
-        copies = exchange_tile(phase, lambda h: stage.at[it, h], lambda h: rs_buf.at[it, h])
-        total = product[0:tile_rows, :]
+            stage[it][c, h] = product[h * tile_rows : (h + 1) * tile_rows, :].astype(RS_TYPES[it])
+        product_own[it, c] = product[0:tile_rows, :]
+        return exchange_tile(
+            (2 * it) * CHUNKS + c,
+            lambda h: stage[it].at[c, h],
+            lambda h: rs_buf[it].at[c, h],
+            chunk_send,
+            chunk_recv,
+        )
+
+    def scatter_sum(it, c, copies):
+        total = product_own[it, c]
         for h, copy in enumerate(copies, 1):
             copy.wait()
-            total = total + rs_buf[it, h].astype(f32)
+            total = total + rs_buf[it][c, h].astype(f32)
         return total
+
+    def gather_send(it, c, vector):
+        ag_mine[it, c] = vector.astype(jnp.bfloat16)
+        return exchange_tile(
+            (2 * it + 1) * CHUNKS + c,
+            lambda h: ag_mine.at[it, c],
+            lambda h: ag_buf.at[it, c, h],
+            chunk_send,
+            chunk_recv,
+        )
 
     def lanes_sum(x):
         x = jnp.sum(x, axis=0, keepdims=True)
         total = x[:, 0:LANES]
-        for c in range(1, width // LANES):
+        for c in range(1, span // LANES):
             total = total + x[:, c * LANES : (c + 1) * LANES]
         return total
 
-    def gather_forward(it, phase, vector, scalars):
-        packed = vector.astype(jnp.bfloat16)
-        ag_mine[it] = packed
-        first = exchange_tile(phase, lambda h: ag_mine.at[it], lambda h: ag_buf.at[it, h])
+    def forward(it, phase, gathers, scalars):
         for i, s in enumerate(scalars):
             sc_mine[it, i : i + 1, :] = s
-        second = exchange_tile(phase + 1, lambda h: sc_mine.at[it], lambda h: sc_buf.at[it, h])
-        blocks[0:tile_rows, :] = packed.astype(f32)
-        for h, copy in enumerate(first, 1):
-            copy.wait()
-            blocks[h * tile_rows : (h + 1) * tile_rows, :] = ag_buf[it, h].astype(f32)
-        out = lax.dot_general(
-            blocks[...].astype(jnp.bfloat16),
-            held[...],
-            (((1,), (1,)), ((), ())),
-            preferred_element_type=f32,
-        )
+        second = exchange_tile(phase, lambda h: sc_mine.at[it], lambda h: sc_buf.at[it, h])
+        out = jnp.zeros((n_block, rows), f32)
+        for c in range(CHUNKS):
+            parts = [ag_mine[it, c].astype(f32)]
+            for h, copy in enumerate(gathers[c], 1):
+                copy.wait()
+                parts.append(ag_buf[it, c, h].astype(f32))
+            out = out + lax.dot_general(
+                jnp.concatenate(parts, axis=0).astype(jnp.bfloat16),
+                held[c],
+                (((1,), (1,)), ((), ())),
+                preferred_element_type=f32,
+            )
         out = jnp.sum(jnp.where(to_fwd, out, jnp.zeros((), f32)), axis=0, keepdims=True)
         cols = []
         per = k * pix // LANES
@@ -210,44 +240,64 @@
 
     start = measured[...]
     left = left_side(start)
-    bands = band * (width // BANDS_PER_GROUP_PIX) + (
-        lax.broadcasted_iota(jnp.int32, (1, width), 1) // BANDS_PER_GROUP_PIX
-    )
-    product = jnp.zeros((n_block, width), f32)
-    for g in range(entries // group):
-        for e in range(g * group, (g + 1) * group):
+    sends = []
+    for c in range(CHUNKS):
+        bands = band * (width // BANDS_PER_GROUP_PIX) + (
+            (c * span + lax.broadcasted_iota(jnp.int32, (1, span), 1)) // BANDS_PER_GROUP_PIX
+        )
+        for e in range(entries):
             t, j = entry_of(e)
-            loads[e].wait()
+            loads[c][e].wait()
             at = pl.ds(e * pix, pix)
             inside = jnp.where(
-                (bands >= window[t, j, 0]) & (bands < window[t, j, 1]), 1.0, 0.0
+                (bands >= window[t, 0, j]) & (bands < window[t, 1, j]), 1.0, 0.0
             ).astype(jnp.bfloat16)
-            held[at, :] = held[at, :] * inside
-        span = group * pix
-        product = product + jnp.dot(
-            left[:, g * span : (g + 1) * span],
-            held[g * span : (g + 1) * span, :],
-            preferred_element_type=f32,
-        )
-    direction = scatter_sum(0, 0, product)
-
-    norm = lanes_sum(direction * direction)
-    image, (gamma, _) = gather_forward(0, 1, direction, [norm])
-    alpha = gamma / (image_square(0, 3, image) + RIDGE * gamma)
-    solved = alpha * direction
+            held[c, at, :] = held[c, at, :] * inside
+        product = jnp.dot(left, held[c], preferred_element_type=f32)
+        if c == 0:
+            pl.semaphore_wait(barrier, n_tile + n_band - 2)
+        sends.append(scatter_send(0, c, product))
+    gathers = []
+    norm = jnp.zeros((1, LANES), f32)
+    for c in range(CHUNKS):
+        direction = scatter_sum(0, c, sends[c])
+        gathers.append(gather_send(0, c, direction))
+        grad_buf[0, c] = direction
+        norm = norm + lanes_sum(direction * direction)
+    image, (gamma, _) = forward(0, 0, gathers, [norm])
+    alpha = gamma / (image_square(0, 1, image) + RIDGE * gamma)
     residual = start - alpha * image
 
-    product = jnp.dot(left_side(residual), held[...], preferred_element_type=f32)
-    gradient = scatter_sum(1, 4, product) - RIDGE * solved
-    partial, (gamma_next, cross) = gather_forward(
-        1, 5, gradient, [lanes_sum(gradient * gradient), lanes_sum(gradient * direction)]
-    )
+    left = left_side(residual)
+    sends = [
+        scatter_send(1, c, jnp.dot(left, held[c], preferred_element_type=f32))
+        for c in range(CHUNKS)
+    ]
+    gathers = []
+    norm, cross = jnp.zeros((1, LANES), f32), jnp.zeros((1, LANES), f32)
+    for c in range(CHUNKS):
+        direction = grad_buf[0, c]
+        gradient = scatter_sum(1, c, sends[c]) - RIDGE * (alpha * direction)
+        gathers.append(gather_send(1, c, gradient))
+        grad_buf[1, c] = gradient
+        norm = norm + lanes_sum(gradient * gradient)
+        cross = cross + lanes_sum(gradient * direction)
+    partial, (gamma_next, cross) = forward(1, 2, gathers, [norm, cross])
     beta = gamma_next / gamma
     image = partial + beta * image
     square = gamma_next + 2.0 * beta * cross + beta * beta * gamma
-    alpha = gamma_next / (image_square(1, 7, image) + RIDGE * square)
-    solution_out[...] = solved + alpha * (gradient + beta * direction)
-    residual_out[...] = residual - alpha * image
+    step = gamma_next / (image_square(1, 3, image) + RIDGE * square)
+    for c in range(CHUNKS):
+        cols = pl.ds(c * span, span)
+        solved_out[:, cols] = alpha * grad_buf[0, c]
+        step_out[:, cols] = step * (grad_buf[1, c] + beta * grad_buf[0, c])
+    residual_out[...] = residual
+    change_out[...] = step * image
+
+
+def finish_kernel(solved, step, residual, change, solution_out, residual_out):
+    solution_out[...] = solved[...] + step[...]
+    residual_out[...] = residual[...] - change[...]
 
 
 def body(calib, support, band_window, measured):
@@ -258,34 +308,45 @@
     f32, bf16 = jnp.float32, jnp.bfloat16
     vmem, smem = pl.BlockSpec(memory_space=pltpu.VMEM), pl.BlockSpec(memory_space=pltpu.SMEM)
     dma = pltpu.SemaphoreType.DMA
-    solved, residual = pl.pallas_call(
-        functools.partial(kernel, n_tile, n_band, 4),
-        out_shape=(
-            jax.ShapeDtypeStruct((tile_rows, width), f32),
-            jax.ShapeDtypeStruct((1, sensor), f32),
-        ),
+    span = width // CHUNKS
+    cube = jax.ShapeDtypeStruct((tile_rows, width), f32)
+    image = jax.ShapeDtypeStruct((1, sensor), f32)
+    held_back = pl.pallas_call(
+        functools.partial(kernel, n_tile, n_band),
+        out_shape=(cube, cube, image, image),
         in_specs=[pl.BlockSpec(memory_space=pl.ANY), smem, smem, vmem],
-        out_specs=(vmem, vmem),
+        out_specs=(vmem,) * 4,
         scratch_shapes=[
-            pltpu.VMEM((entries * pix, width), bf16),
-            pltpu.VMEM((2, n_tile, tile_rows, width), RS_TYPE),
-            pltpu.VMEM((2, n_tile, tile_rows, width), RS_TYPE),
-            pltpu.VMEM((2, tile_rows, width), bf16),
-            pltpu.VMEM((2, n_tile, tile_rows, width), bf16),
+            pltpu.VMEM((CHUNKS, entries * pix, span), bf16),
+            pltpu.VMEM((CHUNKS, n_tile, tile_rows, span), RS_TYPES[0]),
+            pltpu.VMEM((CHUNKS, n_tile, tile_rows, span), RS_TYPES[1]),
+            pltpu.VMEM((CHUNKS, n_tile, tile_rows, span), RS_TYPES[0]),
+            pltpu.VMEM((CHUNKS, n_tile, tile_rows, span), RS_TYPES[1]),
+            pltpu.VMEM((2, CHUNKS, tile_rows, span), f32),
+            pltpu.VMEM((2, CHUNKS, tile_rows, span), f32),
+            pltpu.VMEM((2, CHUNKS, tile_rows, span), bf16),
+            pltpu.VMEM((2, CHUNKS, n_tile, tile_rows, span), bf16),
             pltpu.VMEM((2, 8, LANES), f32),
             pltpu.VMEM((2, n_tile, 8, LANES), f32),
-            pltpu.VMEM((n_tile * tile_rows, width), f32),
             pltpu.VMEM((2, n_band, 8, sensor), f32),
             pltpu.VMEM((2, 8, sensor), f32),
             pltpu.VMEM((2, n_tile, 8, sensor), f32),
-            dma((entries,)),
-            dma((8, n_tile)),
-            dma((8, n_tile)),
+            dma((CHUNKS, entries)),
+            dma((4 * CHUNKS, n_tile)),
+            dma((4 * CHUNKS, n_tile)),
+            dma((4, n_tile)),
+            dma((4, n_tile)),
             dma((2, n_band)),
             dma((2, n_band)),
         ],
         compiler_params=pltpu.CompilerParams(collective_id=0, has_side_effects=True),
-    )(calib, support, band_window, measured.reshape(1, sensor))
+    )(calib, support, jnp.transpose(band_window, (0, 2, 1)), measured.reshape(1, sensor))
+    solved, residual = pl.pallas_call(
+        finish_kernel,
+        out_shape=(cube, image),
+        in_specs=[vmem] * 4,
+        out_specs=(vmem, vmem),
+    )(*held_back)
     return solved, residual.reshape(sensor)
 
 

time: 48.5 us -> 46.9 us (0.967)
  local copies, waits for them, and re-layouts: 3.82 us -> 0 us
  Pallas kernels: 43.7 us -> 46.1 us
    unnamed x3 -> x0, local copies, waits for them, and re-layouts: 3.82 us -> none
    pallas_call x1 -> x2, Pallas kernels: 43.7 us -> 46.1 us  [the longest x1 44.7 us: body(): pl.pallas_call(functools.partial(kernel, n_tile, n_band), out_shape=(cube...]
where the time goes in v2:
time: 46.9 us; the launch traced here: 46.7 us
  Pallas kernels  46.1 us (98%)
  between operations  0.64 us (1%)
    pallas_call x1, Pallas kernels, body(): pl.pallas_call(functools.partial(kernel, n_tile, n_band), out_shape=(cube...  44.7 us
    pallas_call x1, Pallas kernels, body(): pl.pallas_call(finish_kernel, out_shape=(cube, image), in_specs=[vmem] *...  1.35 us

profile of v2, /device:TPU:0, one launch (start us, length us, event | category | flops | bytes accessed | tf_op | source)
XLA Modules:
  0.0 46.7 jit_solution(457260017355131375)
XLA Ops:
  0.6 44.7 %shard_map.59 = (f32[2,2048]{1,0:T(2,128)}, f32[2,2048]{1,0:T(2,128)}, f32[1,128]{1,0:T(1,128)}, f32[1,128]{1,0:T(1,128)}) custom-call(bf16[2,8,64,2048]{3,2,1,0:T(8,128)(2,1)} %calib.1, s32[2,8]{1,0:T(2,128)} %support.1, s32[2,2,8]{2,1,0:T(2,128)} %bitcast.3, f32[1,128]{1,0:T(1,128)} %bitcast.4), custom_call_target="tpu_custom_call" | custom-call | tf_op jit(solution)/shard_map/pallas_call | solution.py:314
  45.3 1.4 %shard_map.60 = (f32[2,2048]{1,0:T(2,128)}, f32[1,128]{1,0:T(1,128)}) custom-call(f32[2,2048]{1,0:T(2,128)} %get-tuple-element.8.solved, f32[2,2048]{1,0:T(2,128)} %get-tuple-element.9.step, f32[1,128]{1,0:T(1,128)} %get-tuple-element.10.residual, f32[1,128]{1,0:T(1,128)} %get-tuple-element.11.change), custom_call_target="tpu_custom_call" | custom-call | tf_op jit(solution)/shard_map/pallas_call | solution.py:344

commit v3 on v2

--- a/solution.py
+++ b/solution.py
@@ -35,18 +35,12 @@
     grad_buf,
     ag_mine,
     ag_buf,
-    sc_mine,
-    sc_buf,
-    band_buf,
-    sq_mine,
-    sq_buf,
+    all_buf,
     load_sem,
     chunk_send,
     chunk_recv,
-    tile_send,
-    tile_recv,
-    band_send,
-    band_recv,
+    all_send,
+    all_recv,
 ):
     tile_rows, k, pix, width = calib.shape
     entries = tile_rows * k
@@ -78,10 +72,14 @@
     barrier = pltpu.get_barrier_semaphore()
     peers = [lax.rem(me + h, n_tile) for h in range(n_tile)]
     others = [lax.rem(band + h, n_band) for h in range(n_band)]
-    for h in range(1, n_tile):
-        pl.semaphore_signal(barrier, inc=1, device_id={"tile": peers[h]}, device_id_type=MESH)
-    for h in range(1, n_band):
-        pl.semaphore_signal(barrier, inc=1, device_id={"band": others[h]}, device_id_type=MESH)
+    everyone = [(a, b) for a in range(n_tile) for b in range(n_band) if a or b]
+    for a, b in everyone:
+        pl.semaphore_signal(
+            barrier,
+            inc=1,
+            device_id={"tile": peers[a], "band": others[b]},
+            device_id_type=MESH,
+        )
 
     lane_entry = lax.broadcasted_iota(jnp.int32, (1, rows), 1) // pix
     sup_row = jnp.zeros((1, rows), jnp.int32)
@@ -99,6 +97,7 @@
 
     lane = lax.broadcasted_iota(jnp.int32, (1, LANES), 1)
     low = lane < pix
+    first_half = lane < LANES // 2
 
     def spread(w):
         pieces = []
@@ -114,7 +113,7 @@
         wide = jnp.broadcast_to(spread(w), (n_block, rows))
         return jnp.where(to_adj, wide, jnp.zeros((), f32)).astype(jnp.bfloat16)
 
-    def exchange_tile(phase, source, target, sends=tile_send, recvs=tile_recv):
+    def exchange_tile(phase, source, target, sends, recvs):
         copies = []
         for h in range(1, n_tile):
             copy = pltpu.make_async_remote_copy(
@@ -129,15 +128,15 @@
             copies.append(copy)
         return copies
 
-    def exchange_band(phase):
+    def exchange_all(it):
         copies = []
-        for h in range(1, n_band):
+        for a, b in everyone:
             copy = pltpu.make_async_remote_copy(
-                src_ref=band_buf.at[phase, band],
-                dst_ref=band_buf.at[phase, band],
-                send_sem=band_send.at[phase, h],
-                recv_sem=band_recv.at[phase, h],
-                device_id={"band": others[h]},
+                src_ref=all_buf.at[it, me, band],
+                dst_ref=all_buf.at[it, me, band],
+                send_sem=all_send.at[it, a, b],
+                recv_sem=all_recv.at[it, a, b],
+                device_id={"tile": peers[a], "band": others[b]},
                 device_id_type=MESH,
             )
             copy.start()
@@ -184,10 +183,7 @@
             total = total + x[:, c * LANES : (c + 1) * LANES]
         return total
 
-    def forward(it, phase, gathers, scalars):
-        for i, s in enumerate(scalars):
-            sc_mine[it, i : i + 1, :] = s
-        second = exchange_tile(phase, lambda h: sc_mine.at[it], lambda h: sc_buf.at[it, h])
+    def forward(it, gathers, scalars):
         out = jnp.zeros((n_block, rows), f32)
         for c in range(CHUNKS):
             parts = [ag_mine[it, c].astype(f32)]
@@ -212,35 +208,31 @@
         image = jnp.concatenate(
             [jnp.where(low, cols[t], cols[t + 1]) for t in range(0, tile_rows, 2)], axis=1
         )
-        finish(second)
-        sums = sc_mine[it]
-        for h in range(1, n_tile):
-            sums = sums + sc_buf[it, h]
-        band_buf[it, band, 0:1, :] = image
-        band_buf[it, band, 1:3, :] = sums[0:2, :]
-        finish(exchange_band(it))
-        total = band_buf[it, 0]
+        halves = [x + pltpu.roll(x, LANES // 2, 1) for x in scalars]
+        all_buf[it, me, band, 0:1, :] = image
+        all_buf[it, me, band, 1:2, :] = jnp.where(first_half, halves[0], halves[1])
+        finish(exchange_all(it))
+        total = all_buf[it, :, 0]
+        mine = all_buf[it, me, 0]
         for b in range(1, n_band):
-            total = total + band_buf[it, b]
-        return total[0:1, :], [jnp.sum(total[i : i + 1, :], axis=1, keepdims=True) for i in (1, 2)]
-
-    def image_square(it, phase, image):
-        sq_mine[it, 0:1, :] = image * image
-        copies = exchange_tile(phase, lambda h: sq_mine.at[it], lambda h: sq_buf.at[it, h])
-        total = image * image
-        for h, copy in enumerate(copies, 1):
-            copy.wait()
-            total = total + sq_buf[it, h, 0:1, :]
-        return jnp.sum(total, axis=1, keepdims=True)
-
-    for it in range(2):
-        sc_mine[it] = jnp.zeros_like(sc_mine[it])
-        sq_mine[it] = jnp.zeros_like(sq_mine[it])
-        band_buf[it, band] = jnp.zeros_like(band_buf[it, band])
+            total = total + all_buf[it, :, b]
+            mine = mine + all_buf[it, me, b]
+        sums = jnp.sum(total, axis=0)[1:2, :]
+        zero = jnp.zeros_like(sums)
+        return (
+            total,
+            mine[0:1, :],
+            jnp.sum(jnp.where(first_half, sums, zero), axis=1, keepdims=True),
+            jnp.sum(jnp.where(first_half, zero, sums), axis=1, keepdims=True),
+        )
+
+    def image_square(total):
+        square = jnp.sum(total * total, axis=0)[0:1, :]
+        return jnp.sum(square, axis=1, keepdims=True)
 
     start = measured[...]
     left = left_side(start)
-    sends = []
+    products = []
     for c in range(CHUNKS):
         bands = band * (width // BANDS_PER_GROUP_PIX) + (
             (c * span + lax.broadcasted_iota(jnp.int32, (1, span), 1)) // BANDS_PER_GROUP_PIX
@@ -254,9 +246,9 @@
             ).astype(jnp.bfloat16)
             held[c, at, :] = held[c, at, :] * inside
         product = jnp.dot(left, held[c], preferred_element_type=f32)
-        if c == 0:
-            pl.semaphore_wait(barrier, n_tile + n_band - 2)
-        sends.append(scatter_send(0, c, product))
+        products.append(product)
+    pl.semaphore_wait(barrier, n_tile * n_band - 1)
+    sends = [scatter_send(0, c, products[c]) for c in range(CHUNKS)]
     gathers = []
     norm = jnp.zeros((1, LANES), f32)
     for c in range(CHUNKS):
@@ -264,8 +256,8 @@
         gathers.append(gather_send(0, c, direction))
         grad_buf[0, c] = direction
         norm = norm + lanes_sum(direction * direction)
-    image, (gamma, _) = forward(0, 0, gathers, [norm])
-    alpha = gamma / (image_square(0, 1, image) + RIDGE * gamma)
+    images, image, gamma, _ = forward(0, gathers, [norm, norm])
+    alpha = gamma / (image_square(images) + RIDGE * gamma)
     residual = start - alpha * image
 
     left = left_side(residual)
@@ -282,11 +274,12 @@
         grad_buf[1, c] = gradient
         norm = norm + lanes_sum(gradient * gradient)
         cross = cross + lanes_sum(gradient * direction)
-    partial, (gamma_next, cross) = forward(1, 2, gathers, [norm, cross])
+    partials, partial, gamma_next, cross = forward(1, gathers, [norm, cross])
     beta = gamma_next / gamma
     image = partial + beta * image
+    images = partials + beta * images
     square = gamma_next + 2.0 * beta * cross + beta * beta * gamma
-    step = gamma_next / (image_square(1, 3, image) + RIDGE * square)
+    step = gamma_next / (image_square(images) + RIDGE * square)
     for c in range(CHUNKS):
         cols = pl.ds(c * span, span)
         solved_out[:, cols] = alpha * grad_buf[0, c]
@@ -326,18 +319,12 @@
             pltpu.VMEM((2, CHUNKS, tile_rows, span), f32),
             pltpu.VMEM((2, CHUNKS, tile_rows, span), bf16),
             pltpu.VMEM((2, CHUNKS, n_tile, tile_rows, span), bf16),
-            pltpu.VMEM((2, 8, LANES), f32),
-            pltpu.VMEM((2, n_tile, 8, LANES), f32),
-            pltpu.VMEM((2, n_band, 8, sensor), f32),
-            pltpu.VMEM((2, 8, sensor), f32),
-            pltpu.VMEM((2, n_tile, 8, sensor), f32),
+            pltpu.VMEM((2, n_tile, n_band, 2, sensor), f32),
             dma((CHUNKS, entries)),
             dma((4 * CHUNKS, n_tile)),
             dma((4 * CHUNKS, n_tile)),
-            dma((4, n_tile)),
-            dma((4, n_tile)),
-            dma((2, n_band)),
-            dma((2, n_band)),
+            dma((2, n_tile, n_band)),
+            dma((2, n_tile, n_band)),
         ],
         compiler_params=pltpu.CompilerParams(collective_id=0, has_side_effects=True),
     )(calib, support, jnp.transpose(band_window, (0, 2, 1)), measured.reshape(1, sensor))

time: 46.9 us -> 44.2 us (0.942)
  Pallas kernels: 46.1 us -> 43.3 us
    pallas_call x1, Pallas kernels: 44.7 us -> 42 us  [body(): pl.pallas_call(functools.partial(kernel, n_tile, n_band), out_shape=(cube...]
where the time goes in v3:
time: 44.2 us; the launch traced here: 44 us
  Pallas kernels  43.3 us (98%)
  between operations  0.64 us (1%)
    pallas_call x1, Pallas kernels, body(): pl.pallas_call(functools.partial(kernel, n_tile, n_band), out_shape=(cube...  42 us
    pallas_call x1, Pallas kernels, body(): pl.pallas_call(finish_kernel, out_shape=(cube, image), in_specs=[vmem] *...  1.35 us

profile of v3, /device:TPU:0, one launch (start us, length us, event | category | flops | bytes accessed | tf_op | source)
XLA Modules:
  0.0 44.0 jit_solution(11546141277859080779)
XLA Ops:
  0.6 42.0 %shard_map.59 = (f32[2,2048]{1,0:T(2,128)}, f32[2,2048]{1,0:T(2,128)}, f32[1,128]{1,0:T(1,128)}, f32[1,128]{1,0:T(1,128)}) custom-call(bf16[2,8,64,2048]{3,2,1,0:T(8,128)(2,1)} %calib.1, s32[2,8]{1,0:T(2,128)} %support.1, s32[2,2,8]{2,1,0:T(2,128)} %bitcast.3, f32[1,128]{1,0:T(1,128)} %bitcast.4), custom_call_target="tpu_custom_call" | custom-call | tf_op jit(solution)/shard_map/pallas_call | solution.py:307
  42.6 1.4 %shard_map.60 = (f32[2,2048]{1,0:T(2,128)}, f32[1,128]{1,0:T(1,128)}) custom-call(f32[2,2048]{1,0:T(2,128)} %get-tuple-element.8.solved, f32[2,2048]{1,0:T(2,128)} %get-tuple-element.9.step, f32[1,128]{1,0:T(1,128)} %get-tuple-element.10.residual, f32[1,128]{1,0:T(1,128)} %get-tuple-element.11.change), custom_call_target="tpu_custom_call" | custom-call | tf_op jit(solution)/shard_map/pallas_call | solution.py:331

commit v4 on v3

--- a/solution.py
+++ b/solution.py
@@ -11,7 +11,7 @@
 RIDGE = 0.25
 LANES = 128
 RS_TYPES = (jnp.float32, jnp.bfloat16)
-CHUNKS = 4
+CHUNKS = 2
 MESH = pl.DeviceIdType.MESH
 
 

time: 44.2 us -> 43.6 us (0.986)
  Pallas kernels: 43.3 us -> 42.7 us
    pallas_call x1, Pallas kernels: 42 us -> 41.4 us  [body(): pl.pallas_call(functools.partial(kernel, n_tile, n_band), out_shape=(cube...]
where the time goes in v4:
time: 43.6 us; the launch traced here: 43.4 us
  Pallas kernels  42.7 us (98%)
  between operations  0.64 us (1%)
    pallas_call x1, Pallas kernels, body(): pl.pallas_call(functools.partial(kernel, n_tile, n_band), out_shape=(cube...  41.4 us
    pallas_call x1, Pallas kernels, body(): pl.pallas_call(finish_kernel, out_shape=(cube, image), in_specs=[vmem] *...  1.35 us

profile of v4, /device:TPU:0, one launch (start us, length us, event | category | flops | bytes accessed | tf_op | source)
XLA Modules:
  0.0 43.4 jit_solution(13808975357933598718)
XLA Ops:
  0.6 41.4 %shard_map.59 = (f32[2,2048]{1,0:T(2,128)}, f32[2,2048]{1,0:T(2,128)}, f32[1,128]{1,0:T(1,128)}, f32[1,128]{1,0:T(1,128)}) custom-call(bf16[2,8,64,2048]{3,2,1,0:T(8,128)(2,1)} %calib.1, s32[2,8]{1,0:T(2,128)} %support.1, s32[2,2,8]{2,1,0:T(2,128)} %bitcast.3, f32[1,128]{1,0:T(1,128)} %bitcast.4), custom_call_target="tpu_custom_call" | custom-call | tf_op jit(solution)/shard_map/pallas_call | solution.py:307
  42.0 1.4 %shard_map.60 = (f32[2,2048]{1,0:T(2,128)}, f32[1,128]{1,0:T(1,128)}) custom-call(f32[2,2048]{1,0:T(2,128)} %get-tuple-element.8.solved, f32[2,2048]{1,0:T(2,128)} %get-tuple-element.9.step, f32[1,128]{1,0:T(1,128)} %get-tuple-element.10.residual, f32[1,128]{1,0:T(1,128)} %get-tuple-element.11.change), custom_call_target="tpu_custom_call" | custom-call | tf_op jit(solution)/shard_map/pallas_call | solution.py:331
